TPU v7x, 32 devices: a whole 2x2x4 slice. The times are simulated.
32 devices in a mesh: dp: 8 (over y, x, core), head: 4 (over z).
Axes of the slice: x: 2, y: 2, z: 4, core: 2. Of those that a mesh axis runs over, the one named last changes fastest.
Arguments:
- tokens: bfloat16 [2048, 2048], P('dp'), may hold values from -6 to 6
- weights: bfloat16 [4, 768, 2048], P('head', 'dp'), may hold values from -0.13479223 to 0.13479223, as said below
- query_gain: float32 [128], replicated, may hold values from 0.25 to 1.75
- key_gain: float32 [128], replicated, may hold values from 0.25 to 1.75
- first_row: int32 [2048], P('dp'), may hold values from 0 to 2047, as said below
- cotangent: bfloat16 [2048, 2048], P('dp', 'head'), may hold values from -6 to 6
Outputs:
- attended: bfloat16 [2048, 2048], P('dp', 'head')
- token_grad: bfloat16 [2048, 2048], P('dp', 'head')
- weight_grad: float32 [4, 768, 2048], P('head', 'dp')
Inputs may be any that keep to these rules, and one draw needn't show every extreme that they name: first_row[i] is the position of the first row of row i's document: documents are runs of consecutive rows, each at most 512 rows long, one of exactly 512 rows, and the last row begins a document of its own. For every even g, weights[g] and weights[g + 1] are equal in their last 256 rows: each key-value head is held by two head devices.
All inputs are finite; a program needn't handle non-finite values.
Results may differ from a plain program's by a relative error of at most 0.017.
Values may be sent and summed in bfloat16 or wider, within the bound.
No kernel may reach another device: no remote copies, remote signals or barrier semaphores. Data moves between devices by JAX's collectives and lax.ppermute only.
A program may use at most 64 MiB of HBM per device.

v0:
```python
import math
import jax
import jax.numpy as jnp
from jax import lax
from jax.sharding import PartitionSpec as P

HD = 128
QH_DEV = 4
COLS = 768
ROWS = 256
SPAN = 2
EPSILON = 1e-06
THETA = 1000000.0
STRETCH = 0.25


def from_behind(x, axis, by):
    devices = lax.axis_size(axis)
    pairs = [(i, i + by) for i in range(devices) if 0 <= i + by < devices]
    return lax.ppermute(x, axis, pairs)


def partner(x, axis, apart):
    return lax.ppermute(x, axis, [(i, i ^ 1 << apart) for i in range(lax.axis_size(axis))])


def rope_tables(position, head_size):
    middle = head_size // 2
    channel = jnp.arange(middle, dtype=jnp.float32)
    frequency = THETA ** (-2.0 * channel / head_size)
    angles = (position.astype(jnp.float32) * STRETCH)[:, None] * frequency[None, :]
    angles = jnp.concatenate([angles, angles], axis=1)
    return (jnp.cos(angles), jnp.sin(angles))


def normalize_rotate(values, scaling, cosine_table, sine_table):
    factor = lax.rsqrt(jnp.mean(values * values, axis=-1, keepdims=True) + EPSILON)
    normed = values * factor * scaling
    middle = normed.shape[-1] // 2
    turned = jnp.concatenate([-normed[..., middle:], normed[..., :middle]], axis=-1)
    return normed * cosine_table + turned * sine_table


def prepare(projected, query_gain, key_gain, cosine_table, sine_table):
    row_count = projected.shape[0]
    queries = projected[:, : QH_DEV * HD].reshape(row_count, QH_DEV, HD)
    queries = normalize_rotate(
        queries, query_gain, cosine_table[:, None, :], sine_table[:, None, :]
    )
    key_part = normalize_rotate(
        projected[:, QH_DEV * HD : (QH_DEV + 1) * HD], key_gain, cosine_table, sine_table
    )
    value_part = projected[:, (QH_DEV + 1) * HD :]
    return (queries, key_part, value_part)


def attend_window(queries, window, upstream, first_rows, query_place, key_place):
    score_scale = 1.0 / math.sqrt(HD)
    key_window = window[:, :HD]
    value_window = window[:, HD:]
    visible = (key_place[None, :] >= first_rows[:, None]) & (
        key_place[None, :] <= query_place[:, None]
    )
    score = (
        jnp.einsum("rhc,kc->rhk", queries, key_window, preferred_element_type=jnp.float32)
        * score_scale
    )
    weight = jnp.where(visible[:, None, :], jnp.exp(score), 0.0)
    denominator = jnp.sum(weight, axis=-1)
    summed = jnp.einsum(
        "rhk,kc->rhc", weight.astype(jnp.bfloat16), value_window, preferred_element_type=jnp.float32
    )
    attended = (summed / denominator[..., None]).astype(jnp.bfloat16)
    probability = weight / denominator[..., None]
    row_delta = jnp.sum(upstream.astype(jnp.float32) * attended.astype(jnp.float32), axis=-1)
    grad_prob = jnp.einsum(
        "rhc,kc->rhk", upstream, value_window, preferred_element_type=jnp.float32
    )
    grad_score = (probability * (grad_prob - row_delta[..., None]) * score_scale).astype(
        jnp.bfloat16
    )
    grad_query = jnp.einsum(
        "rhk,kc->rhc", grad_score, key_window, preferred_element_type=jnp.float32
    )
    grad_key = jnp.einsum("rhk,rhc->kc", grad_score, queries, preferred_element_type=jnp.float32)
    grad_value = jnp.einsum(
        "rhk,rhc->kc",
        probability.astype(jnp.bfloat16),
        upstream,
        preferred_element_type=jnp.float32,
    )
    return (attended, grad_query, jnp.concatenate([grad_key, grad_value], axis=1))


def body(tokens, weights, query_gain, key_gain, first_row, cotangent):
    block_index = lax.axis_index("dp")
    position = block_index * ROWS + jnp.arange(ROWS, dtype=jnp.int32)
    key_place = (block_index - SPAN) * ROWS + jnp.arange((SPAN + 1) * ROWS, dtype=jnp.int32)
    cosine_table, sine_table = rope_tables(position, HD)
    weight_piece = lax.all_gather(weights, "dp", axis=1, tiled=True)
    projected = jnp.einsum("rd,cd->rc", tokens, weight_piece[0], preferred_element_type=jnp.float32)
    prepared, pullback = jax.vjp(
        lambda values: prepare(values, query_gain, key_gain, cosine_table, sine_table), projected
    )
    queries = prepared[0].astype(jnp.bfloat16)
    key_value = jnp.concatenate([prepared[1], prepared[2]], axis=1).astype(jnp.bfloat16)
    earlier = [from_behind(key_value, "dp", distance) for distance in range(SPAN, 0, -1)]
    window = jnp.concatenate(earlier + [key_value], axis=0)
    upstream = cotangent.reshape(ROWS, QH_DEV, HD)
    attended, grad_query, slot_grads = attend_window(
        queries, window, upstream, first_row, position, key_place
    )
    pair_grad = slot_grads[SPAN * ROWS :]
    for distance in range(1, SPAN + 1):
        slot_index = SPAN - distance
        pair_grad = pair_grad + from_behind(
            slot_grads[slot_index * ROWS : (slot_index + 1) * ROWS].astype(jnp.bfloat16),
            "dp",
            -distance,
        ).astype(jnp.float32)
    grad_projected = pullback((grad_query, pair_grad[:, :HD], pair_grad[:, HD:]))[0].astype(
        jnp.bfloat16
    )
    partial_grad = jnp.dot(grad_projected, weight_piece[0], preferred_element_type=jnp.float32)
    token_grad = lax.psum_scatter(
        partial_grad.astype(jnp.bfloat16), "head", scatter_dimension=1, tiled=True
    )
    shard_rows = COLS // lax.axis_size("dp")
    own_grad = lax.psum_scatter(
        jnp.einsum("rc,rd->cd", grad_projected, tokens, preferred_element_type=jnp.float32),
        "dp",
        scatter_dimension=0,
        tiled=True,
    )
    partner_grad = partner(own_grad.astype(jnp.bfloat16), "head", 0).astype(own_grad.dtype)
    global_rows = block_index * shard_rows + jnp.arange(shard_rows, dtype=jnp.int32)
    shared_rows = global_rows >= QH_DEV * HD
    weight_grad = jnp.where(shared_rows[:, None], own_grad + partner_grad, own_grad)
    return (attended.reshape(ROWS, QH_DEV * HD), token_grad, weight_grad[None])


def solution(mesh):
    in_specs = (P("dp", None), P("head", "dp", None), P(), P(), P("dp"), P("dp", "head"))
    out_specs = (P("dp", "head"), P("dp", "head"), P("head", "dp", None))
    return jax.shard_map(body, mesh=mesh, in_specs=in_specs, out_specs=out_specs, check_vma=False)
```

profile of v0, /device:TPU:0, one launch (start us, length us, event | category | flops | bytes accessed | tf_op | source)
XLA Modules:
  0.0 185.5 jit_solution(12164193166599489742)
XLA Ops:
  7.2 0.7 all-gather.2.cloned.1.call-update
  8.0 1.8 copy.66
  9.9 1.6 compare_and_fusion
  11.5 33.3 %all-gather.2.cloned.1.call-done = bf16[1,768,2048]{2,1,0:T(8,128)(2,1)} async-done(((bf16[1,96,2048]{2,1,0:T(8,128)(2,1)}), bf16[1,768,2048]{2,1,0:T(8,128)(2,1)}) %all-gather.2.cloned.1.call-update) | async-done | bytes 3145744 | tf_op jit(solution)/shard_map/all_gather | solution.py:100
  44.8 2.9 %fusion.4 = f32[256,768]{1,0:T(8,128)S(1)} fusion(bf16[256,2048]{1,0:T(8,128)(2,1)S(1)} %copy-done, bf16[1,768,2048]{2,1,0:T(8,128)(2,1)} %all-gather.2.cloned.1.call-done), kind=kOutput, calls=%fused_computation.5 | convolution fusion | flops 805306368 | bytes 4980736 | tf_op jit(solution)/shard_map/rd,cd->rc/dot_general | solution.py:101
  48.1 1.3 fusion.39
  49.4 0.7 pad_maximum_fusion.2
  50.0 2.8 %collective-permute-start.1 = (bf16[256,256]{1,0:T(8,128)(2,1)}, bf16[256,256]{1,0:T(8,128)(2,1)}, u32[]{:S(2)}, u32[]{:S(2)}) collective-permute-start(bf16[256,256]{1,0:T(8,128)(2,1)} %pad_maximum_fusion.2), channel_id=1, source_target_pairs={{0,4},{4,8},{8,12},{12,16},{16,20},{20,24},{24,28},{1,5},{5,9},{9,... | collective-permute-start | bytes 393224 | tf_op jit(solution)/shard_map/ppermute | solution.py:20
  52.8 3.4 %collective-permute-start = (bf16[256,256]{1,0:T(8,128)(2,1)}, bf16[256,256]{1,0:T(8,128)(2,1)}, u32[]{:S(2)}, u32[]{:S(2)}) collective-permute-start(bf16[256,256]{1,0:T(8,128)(2,1)} %pad_maximum_fusion.2), channel_id=1, source_target_pairs={{0,8},{4,12},{8,16},{12,20},{16,24},{20,28},{1,9},{5,13},{9,17},{1... | collective-permute-start | bytes 393224 | tf_op jit(solution)/shard_map/ppermute | solution.py:20
  57.0 1.0 copy.63
  58.6 0.9 collective-permute-done
  59.5 1.0 maximum_maximum_fusion
  60.5 1.0 fusion.10
  61.6 1.4 multiply_reduce_fusion.1
  63.0 1.1 fusion.19
  64.1 1.5 fusion.1
  66.2 0.7 broadcast_multiply_fusion
  67.1 0.7 fusion.50
  67.8 1.3 collective-permute-start.2
  69.1 1.3 collective-permute-start.3
  71.4 7.2 %collective-permute-done.3 = bf16[256,256]{1,0:T(8,128)(2,1)} collective-permute-done((bf16[256,256]{1,0:T(8,128)(2,1)}, bf16[256,256]{1,0:T(8,128)(2,1)}, u32[]{:S(2)}, u32[]{:S(2)}) %collective-permute-start.3) | collective-permute-done | bytes 131104 | tf_op jit(solution)/shard_map/ppermute | solution.py:20
  78.6 1.1 fusion.35
  80.3 0.6 multiply_reduce_fusion.3
  81.1 3.7 %fusion.48 = f32[768,2048]{1,0:T(8,128)} fusion(bf16[256,2048]{1,0:T(8,128)(2,1)S(1)} %copy-done, f32[256,512]{1,0:T(8,128)S(1)} %copy.87, f32[256,128]{1,0:T(8,128)S(1)} %add_add_fusion.1, f32[256,128]{1,0:T(8,128)S(1)} %get-tuple-element.23), kind=kOutput, calls=%fused_computation.82 | convolution fusion | flops 805896192 | bytes 8126464 | tf_op jit(solution)/shard_map/rc,rd->cd/dot_general | solution.py:130
  84.9 3.9 %fusion.6 = bf16[256,2048]{1,0:T(8,128)(2,1)} fusion(bf16[1,768,2048]{2,1,0:T(8,128)(2,1)} %all-gather.2.cloned.1.call-done, f32[256,512]{1,0:T(8,128)S(1)} %copy.87, f32[256,128]{1,0:T(8,128)S(1)} %add_add_fusion.1, f32[256,128]{1,0:T(8,128)S(1)} %get-tuple-element.23), kind=kOutput, calls=%fused_computation.8 | convolution fusion | flops 806420480 | bytes 4980736 | tf_op jit(solution)/shard_map/dot_general | solution.py:124
  88.8 59.1 %reduce-scatter.5.cloned.1.call-done = f32[96,2048]{1,0:T(8,128)} async-done(((f32[768,2048]{1,0:T(8,128)}), f32[96,2048]{1,0:T(8,128)}) %reduce-scatter.5.cloned.1.call-update) | async-done | bytes 786448 | tf_op jit(solution)/shard_map/reduce_scatter | solution.py:129
  147.9 1.2 convert_element_type.61
  149.1 1.6 collective-permute-start.4
  150.6 0.8 copy.75
  151.5 11.0 %collective-permute-done.4 = bf16[96,2048]{1,0:T(8,128)(2,1)S(1)} collective-permute-done((bf16[96,2048]{1,0:T(8,128)(2,1)S(1)}, bf16[96,2048]{1,0:T(8,128)(2,1)S(1)}, u32[]{:S(2)}, u32[]{:S(2)}) %collective-permute-start.4) | collective-permute-done | bytes 393248 | tf_op jit(solution)/shard_map/ppermute | solution.py:24
  162.5 2.2 %fusion.29 = f32[1,96,2048]{2,1,0:T(8,128)} fusion(f32[96,2048]{1,0:T(8,128)} %reduce-scatter.5.cloned.1.call-done, bf16[96,2048]{1,0:T(8,128)(2,1)S(1)} %collective-permute-done.4, pred[96]{0:T(512)(128)(4,1)S(1)} %add_compare_fusion), kind=kLoop, calls=%fused_computation.27 | loop fusion | flops 589824 | bytes 1966176 | tf_op jit(solution)/shard_map/broadcast_in_dim | solution.py:139
  164.7 14.3 %reduce-scatter.3.cloned.1.call-done = bf16[256,512]{1,0:T(8,128)(2,1)} async-done(((bf16[256,2048]{1,0:T(8,128)(2,1)}), bf16[256,512]{1,0:T(8,128)(2,1)}) %reduce-scatter.3.cloned.1.call-update) | async-done | bytes 262160 | tf_op jit(solution)/shard_map/reduce_scatter | solution.py:125
  (53 shorter events, 4.5 us)
Async XLA Ops:
  7.2 37.7 %copy-start = (bf16[256,2048]{1,0:T(8,128)(2,1)S(1)}, bf16[256,2048]{1,0:T(8,128)(2,1)}, u32[]{:S(2)}) copy-start(bf16[256,2048]{1,0:T(8,128)(2,1)} %param.6) | copy-start | bytes 3145732
  7.2 37.6 %all-gather.2.cloned.1.call-start = ((), (), s32[]{:S(2)}) async-start(), calls=%async_computation.2 | async-start | bytes 3538944 | tf_op jit(solution)/shard_map/all_gather | solution.py:100
  7.9 140.0 %reduce-scatter.5.cloned.1.call-start = ((), (), s32[]{:S(2)}) async-start(), calls=%async_computation.4 | async-start | bytes 7077888 | tf_op jit(solution)/shard_map/reduce_scatter | solution.py:129
  9.8 38.1 %copy-start.6 = (f32[128]{0:T(128)S(1)}, f32[128]{0:T(128)}, u32[]{:S(2)}) copy-start(f32[128]{0:T(128)} %param.9) | copy-start | bytes 1540
  47.9 10.4 %copy-start.5 = (f32[128]{0:T(128)S(1)}, f32[128]{0:T(128)}, u32[]{:S(2)}) copy-start(f32[128]{0:T(128)} %param.8) | copy-start | bytes 1540
  50.0 8.5 %collective-permute-start.1 = (bf16[256,256]{1,0:T(8,128)(2,1)}, bf16[256,256]{1,0:T(8,128)(2,1)}, u32[]{:S(2)}, u32[]{:S(2)}) collective-permute-start(bf16[256,256]{1,0:T(8,128)(2,1)} %pad_maximum_fusion.2), channel_id=1, source_target_pairs={{0,4},{4,8},{8,12},{12,16},{16,20},{20,24},{24,28},{1,5},{5,9},{9,... | collective-permute-start | bytes 393224 | tf_op jit(solution)/shard_map/ppermute | solution.py:20
  52.8 6.7 %collective-permute-start = (bf16[256,256]{1,0:T(8,128)(2,1)}, bf16[256,256]{1,0:T(8,128)(2,1)}, u32[]{:S(2)}, u32[]{:S(2)}) collective-permute-start(bf16[256,256]{1,0:T(8,128)(2,1)} %pad_maximum_fusion.2), channel_id=1, source_target_pairs={{0,8},{4,12},{8,16},{12,20},{16,24},{20,28},{1,9},{5,13},{9,17},{1... | collective-permute-start | bytes 393224 | tf_op jit(solution)/shard_map/ppermute | solution.py:20
  58.2 2.3 %copy-start.4 = (pred[256,768]{1,0:T(8,128)(4,1)S(1)}, pred[256,768]{1,0:T(8,128)(4,1)}, u32[]{:S(2)}) copy-start(pred[256,768]{1,0:T(8,128)(4,1)} %compare_and_fusion) | copy-start | bytes 589828
  58.4 3.1 %copy-start.3 = (bf16[256,512]{0,1:T(8,128)(2,1)S(1)}, bf16[256,512]{0,1:T(8,128)(2,1)}, u32[]{:S(2)}) copy-start(bf16[256,512]{0,1:T(8,128)(2,1)} %copy.66) | copy-start | bytes 786436
  64.1 3.0 %copy-start.1 = (f32[768,128]{1,0:T(8,128)}, f32[768,128]{1,0:T(8,128)S(1)}, u32[]{:S(2)}) copy-start(f32[768,128]{1,0:T(8,128)S(1)} %fusion.19) | copy-start | bytes 1179652
  67.8 3.6 %collective-permute-start.2 = (bf16[256,256]{1,0:T(8,128)(2,1)}, bf16[256,256]{1,0:T(8,128)(2,1)}, u32[]{:S(2)}, u32[]{:S(2)}) collective-permute-start(bf16[256,256]{1,0:T(8,128)(2,1)} %get-tuple-element.21), channel_id=1, source_target_pairs={{4,0},{8,4},{12,8},{16,12},{20,16},{24,20},{28,24},{5,1},{9,5},{13... | collective-permute-start | bytes 393224 | tf_op jit(solution)/shard_map/ppermute | solution.py:20
  69.1 9.5 %collective-permute-start.3 = (bf16[256,256]{1,0:T(8,128)(2,1)}, bf16[256,256]{1,0:T(8,128)(2,1)}, u32[]{:S(2)}, u32[]{:S(2)}) collective-permute-start(bf16[256,256]{1,0:T(8,128)(2,1)} %get-tuple-element.22), channel_id=1, source_target_pairs={{8,0},{12,4},{16,8},{20,12},{24,16},{28,20},{9,1},{13,5},{17,9},{2... | collective-permute-start | bytes 393224 | tf_op jit(solution)/shard_map/ppermute | solution.py:20
  84.8 65.8 %copy-start.2 = (bf16[256,4,128]{0,2,1:T(8,128)(2,1)S(1)}, bf16[256,4,128]{0,2,1:T(8,128)(2,1)}, u32[]{:S(2)}) copy-start(bf16[256,4,128]{0,2,1:T(8,128)(2,1)} %get-tuple-element.35) | copy-start | bytes 786436
  84.8 94.1 %reduce-scatter.3.cloned.1.call-start = ((), (), s32[]{:S(2)}) async-start(), calls=%async_computation.3 | async-start | bytes 1310720 | tf_op jit(solution)/shard_map/reduce_scatter | solution.py:125
  149.1 13.5 %collective-permute-start.4 = (bf16[96,2048]{1,0:T(8,128)(2,1)S(1)}, bf16[96,2048]{1,0:T(8,128)(2,1)S(1)}, u32[]{:S(2)}, u32[]{:S(2)}) collective-permute-start(bf16[96,2048]{1,0:T(8,128)(2,1)S(1)} %convert_element_type.61), channel_id=1, source_target_pairs={{0,1},{1,0},{2,3},{3,2},{4,5},{5,4},{6,7},{7,6},{8,9},{9,8},{10,11... | collective-permute-start | bytes 1179656 | tf_op jit(solution)/shard_map/ppermute | solution.py:24
Sparse Core Ops, SparseCore 0:
  9.9 34.8 all-gather.1
  84.9 62.8 reduce-scatter.4
  150.8 28.1 reduce-scatter.2
where the time goes:
time: 186 us
  waiting for transfers between devices  127 us (68%)
  matrix products  16.7 us (9%)
  between operations  14.1 us (8%)
  other arithmetic  11.9 us (6%)
  starting transfers between devices  10.4 us (6%)
  local copies, waits for them, and re-layouts  5.22 us (3%)
    reduce_scatter x1, waiting for transfers between devices, body(): lax.psum_scatter(jnp.einsum('rc,rd->cd', grad_projected, tokens, preferre...  59.1 us
    all_gather x1, waiting for transfers between devices, body(): weight_piece = lax.all_gather(weights, 'dp', axis=1, tiled=True)  33.3 us
    reduce_scatter x1, waiting for transfers between devices, body(): lax.psum_scatter(partial_grad.astype(jnp.bfloat16), 'head', scatter_dimen...  14.3 us
    ppermute x1, waiting for transfers between devices, partner(): lax.ppermute(x, axis, [(i, i ^ 1 << apart) for i in range(lax.axis_size(a...  11 us
    ppermute x4, starting transfers between devices, from_behind(): return lax.ppermute(x, axis, pairs)  8.74 us
    ppermute x4, waiting for transfers between devices, from_behind(): return lax.ppermute(x, axis, pairs)  8.71 us
    dot_general x1, matrix products, body(): jnp.dot(grad_projected, weight_piece[0], preferred_element_type=jnp.float32)  3.86 us
  transfers between devices with their start and end apart: 8, of which 7 were waited for; matrix products, arithmetic and copies ran while one was open for 8% of the time, Pallas kernels for 0%

commit v1 on v0

--- a/solution.py
+++ b/solution.py
@@ -97,7 +97,16 @@
     position = block_index * ROWS + jnp.arange(ROWS, dtype=jnp.int32)
     key_place = (block_index - SPAN) * ROWS + jnp.arange((SPAN + 1) * ROWS, dtype=jnp.int32)
     cosine_table, sine_table = rope_tables(position, HD)
-    weight_piece = lax.all_gather(weights, "dp", axis=1, tiled=True)
+    item_now, b_next = (jax.lax.axis_size("dp"), jax.lax.axis_index("dp"))
+    weight_piece, work_now = (weights, 1)
+    while work_now < item_now:
+        front = jax.lax.ppermute(
+            weight_piece, axis_name="dp", perm=[(u, u ^ work_now) for u in range(item_now)]
+        )
+        current_value = jnp.concatenate([weight_piece, front], 1)
+        a_now = jnp.concatenate([front, weight_piece], 1)
+        weight_piece = jnp.where(b_next & work_now == 0, current_value, a_now)
+        work_now = 2 * work_now
     projected = jnp.einsum("rd,cd->rc", tokens, weight_piece[0], preferred_element_type=jnp.float32)
     prepared, pullback = jax.vjp(
         lambda values: prepare(values, query_gain, key_gain, cosine_table, sine_table), projected

time: 186 us -> 206 us (1.11)
  waiting for transfers between devices: 127 us -> 144 us
  starting transfers between devices: 10.4 us -> 14.7 us
    ppermute x0 -> x3, waiting for transfers between devices: none -> 51.5 us  [body(): jax.lax.ppermute(weight_piece, axis_name='dp', perm=[(u, u ^ work_now) fo...]
    all_gather x1 -> x0, waiting for transfers between devices: 33.3 us -> none  [body(): weight_piece = lax.all_gather(weights, 'dp', axis=1, tiled=True)]
    select_n x0 -> x4, other arithmetic: none -> 5.92 us  [body(): weight_piece = jnp.where(b_next & work_now == 0, current_value, a_now)]
    ppermute x0 -> x3, starting transfers between devices: none -> 5.18 us  [body(): jax.lax.ppermute(weight_piece, axis_name='dp', perm=[(u, u ^ work_now) fo...]
  transfers between devices with their start and end apart: 8 -> 10, of which waited for: 7 -> 9; matrix products, arithmetic and copies ran while one was open for 8% -> 6% of each run, Pallas kernels for 0% -> 0%
where the time goes in v1:
time: 206 us
  waiting for transfers between devices  144 us (70%)
  matrix products  16.6 us (8%)
  starting transfers between devices  14.7 us (7%)
  between operations  14.4 us (7%)
  other arithmetic  12.5 us (6%)
  local copies, waits for them, and re-layouts  3.32 us (2%)
    reduce_scatter x1, waiting for transfers between devices, body(): lax.psum_scatter(jnp.einsum('rc,rd->cd', grad_projected, tokens, preferre...  57.9 us
    ppermute x3, waiting for transfers between devices, body(): jax.lax.ppermute(weight_piece, axis_name='dp', perm=[(u, u ^ work_now) fo...  51.5 us
    reduce_scatter x1, waiting for transfers between devices, body(): lax.psum_scatter(partial_grad.astype(jnp.bfloat16), 'head', scatter_dimen...  14.3 us
    ppermute x4, waiting for transfers between devices, from_behind(): return lax.ppermute(x, axis, pairs)  10.6 us
    ppermute x1, waiting for transfers between devices, partner(): lax.ppermute(x, axis, [(i, i ^ 1 << apart) for i in range(lax.axis_size(a...  10.1 us
    ppermute x4, starting transfers between devices, from_behind(): return lax.ppermute(x, axis, pairs)  7.88 us
    select_n x4, other arithmetic, body(): weight_piece = jnp.where(b_next & work_now == 0, current_value, a_now)  5.92 us
    ppermute x3, starting transfers between devices, body(): jax.lax.ppermute(weight_piece, axis_name='dp', perm=[(u, u ^ work_now) fo...  5.18 us
  transfers between devices with their start and end apart: 10, of which 9 were waited for; matrix products, arithmetic and copies ran while one was open for 6% of the time, Pallas kernels for 0%

profile of v1, /device:TPU:0, one launch (start us, length us, event | category | flops | bytes accessed | tf_op | source)
XLA Modules:
  0.0 205.9 jit_solution(18116713539613254351)
XLA Ops:
  7.8 1.6 collective-permute-done
  9.3 2.2 %maximum_select_fusion.4 = bf16[1,192,2048]{2,1,0:T(8,128)(2,1)} fusion(bf16[1,96,2048]{2,1,0:T(8,128)(2,1)S(1)} %collective-permute-done, bf16[1,96,2048]{2,1,0:T(8,128)(2,1)} %param.7, pred[]{:T(512)S(6)} %eq.11), kind=kLoop, calls=%fused_computation.29 | loop fusion | flops 3538944 | bytes 1572865 | tf_op jit(solution)/shard_map/jit(_where)/select_n | solution.py:108
  11.6 2.8 %collective-permute-start.1 = (bf16[1,192,2048]{2,1,0:T(8,128)(2,1)}, bf16[1,192,2048]{2,1,0:T(8,128)(2,1)S(1)}, u32[]{:S(2)}, u32[]{:S(2)}) collective-permute-start(bf16[1,192,2048]{2,1,0:T(8,128)(2,1)} %maximum_select_fusion.4), channel_id=1, source_target_pairs={{0,8},{4,12},{8,0},{12,4},{16,24},{20,28},{24,16},{28,20},{1,9},{5... | collective-permute-start | bytes 2359304 | tf_op jit(solution)/shard_map/ppermute | solution.py:103
  14.4 1.4 maximum_select_fusion.3
  15.8 16.7 %collective-permute-done.1 = bf16[1,192,2048]{2,1,0:T(8,128)(2,1)S(1)} collective-permute-done((bf16[1,192,2048]{2,1,0:T(8,128)(2,1)}, bf16[1,192,2048]{2,1,0:T(8,128)(2,1)S(1)}, u32[]{:S(2)}, u32[]{:S(2)}) %collective-permute-start.1) | collective-permute-done | bytes 786464 | tf_op jit(solution)/shard_map/ppermute | solution.py:103
  32.5 1.7 maximum_select_fusion.2
  34.2 1.8 collective-permute-start.2
  36.5 0.6 maximum_select_fusion.1
  37.1 33.3 %collective-permute-done.2 = bf16[1,384,2048]{2,1,0:T(8,128)(2,1)} collective-permute-done((bf16[1,384,2048]{2,1,0:T(8,128)(2,1)}, bf16[1,384,2048]{2,1,0:T(8,128)(2,1)}, u32[]{:S(2)}, u32[]{:S(2)}) %collective-permute-start.2) | collective-permute-done | bytes 1572896 | tf_op jit(solution)/shard_map/ppermute | solution.py:103
  70.4 2.9 %convolution_bitcast_fusion = f32[256,768]{0,1:T(8,128)S(1)} fusion(bf16[256,2048]{1,0:T(8,128)(2,1)S(1)} %copy-done, bf16[384,2048]{1,0:T(8,128)(2,1)} %bitcast.4, bf16[384,2048]{1,0:T(8,128)(2,1)S(1)} %maximum_select_fusion.1, pred[]{:T(512)S(6)} %eq.9), kind=kOutput, calls=%fused_computation.17 | convolution fusion | flops 819462144 | bytes 4980737 | tf_op jit(solution)/shard_map/rd,cd->rc/dot_general | solution.py:110
  74.1 1.3 collective-permute-start.4
  75.4 4.0 %collective-permute-start.3 = (bf16[256,256]{0,1:T(8,128)(2,1)S(1)}, bf16[256,256]{0,1:T(8,128)(2,1)S(1)}, u32[]{:S(2)}, u32[]{:S(2)}) collective-permute-start(bf16[256,256]{0,1:T(8,128)(2,1)S(1)} %pad_maximum_fusion.2), channel_id=1, source_target_pairs={{0,8},{4,12},{8,16},{12,20},{16,24},{20,28},{1,9},{5,13},{9,17},{1... | collective-permute-start | bytes 393224 | tf_op jit(solution)/shard_map/ppermute | solution.py:20
  79.8 2.9 %collective-permute-done.3 = bf16[256,256]{0,1:T(8,128)(2,1)S(1)} collective-permute-done((bf16[256,256]{0,1:T(8,128)(2,1)S(1)}, bf16[256,256]{0,1:T(8,128)(2,1)S(1)}, u32[]{:S(2)}, u32[]{:S(2)}) %collective-permute-start.3) | collective-permute-done | bytes 131104 | tf_op jit(solution)/shard_map/ppermute | solution.py:20
  82.7 1.1 fusion.3
  83.7 1.5 multiply_reduce_fusion.1
  85.2 1.0 fusion.12
  86.3 1.4 fusion.1
  88.1 0.6 broadcast_multiply_fusion
  89.0 1.3 collective-permute-start.5
  90.3 1.3 collective-permute-start.6
  91.8 0.7 collective-permute-done.5
  92.5 7.0 %collective-permute-done.6 = bf16[256,256]{0,1:T(8,128)(2,1)S(1)} collective-permute-done((bf16[256,256]{0,1:T(8,128)(2,1)S(1)}, bf16[256,256]{0,1:T(8,128)(2,1)S(1)}, u32[]{:S(2)}, u32[]{:S(2)}) %collective-permute-start.6) | collective-permute-done | bytes 131104 | tf_op jit(solution)/shard_map/ppermute | solution.py:20
  101.0 3.6 %fusion.43 = f32[768,2048]{1,0:T(8,128)} fusion(bf16[256,2048]{1,0:T(8,128)(2,1)S(1)} %copy-done, f32[256,512]{0,1:T(8,128)S(1)} %bitcast.56, f32[256,128]{0,1:T(8,128)S(1)} %add_add_fusion.1, f32[256,128]{0,1:T(8,128)S(1)} %get-tuple-element.12), kind=kOutput, calls=%fused_computation.86 | convolution fusion | flops 805896192 | bytes 8126464 | tf_op jit(solution)/shard_map/rc,rd->cd/dot_general | solution.py:139
  104.7 1.3 copy-done.2
  106.0 4.0 %convolution_convert_fusion = bf16[256,2048]{1,0:T(8,128)(2,1)} fusion(bf16[384,2048]{1,0:T(8,128)(2,1)} %bitcast.4, bf16[384,2048]{1,0:T(8,128)(2,1)S(1)} %copy-done.2, pred[]{:T(512)S(6)} %eq.9, f32[256,512]{0,1:T(8,128)S(1)} %bitcast.57, f32[256,128]{0,1:T(8,128)S(1)} %add_add_fusion.1, f32[256,128]{0,1:T(8,128)S(1)} %get-tuple-element.12), kind=kOutput, calls=%fused_computation.5 | convolution fusion | flops 820576256 | bytes 4980737 | tf_op jit(solution)/shard_map/dot_general | solution.py:133
  110.1 57.9 %reduce-scatter.5.cloned.1.call-done = f32[96,2048]{1,0:T(8,128)} async-done(((f32[768,2048]{1,0:T(8,128)}), f32[96,2048]{1,0:T(8,128)}) %reduce-scatter.5.cloned.1.call-update) | async-done | bytes 786448 | tf_op jit(solution)/shard_map/reduce_scatter | solution.py:138
  168.0 1.2 convert_element_type.61
  169.2 1.6 collective-permute-start.7
  170.8 1.8 copy.15
  172.6 10.1 %collective-permute-done.7 = bf16[96,2048]{1,0:T(8,128)(2,1)S(1)} collective-permute-done((bf16[96,2048]{1,0:T(8,128)(2,1)S(1)}, bf16[96,2048]{1,0:T(8,128)(2,1)S(1)}, u32[]{:S(2)}, u32[]{:S(2)}) %collective-permute-start.7) | collective-permute-done | bytes 393248 | tf_op jit(solution)/shard_map/ppermute | solution.py:24
  182.7 2.2 %fusion.22 = f32[1,96,2048]{2,1,0:T(8,128)} fusion(f32[96,2048]{1,0:T(8,128)} %reduce-scatter.5.cloned.1.call-done, bf16[96,2048]{1,0:T(8,128)(2,1)S(1)} %collective-permute-done.7, pred[96]{0:T(512)(128)(4,1)S(1)} %add_compare_fusion), kind=kLoop, calls=%fused_computation.27 | loop fusion | flops 589824 | bytes 1966176 | tf_op jit(solution)/shard_map/broadcast_in_dim | solution.py:148
  184.8 14.3 %reduce-scatter.3.cloned.1.call-done = bf16[256,512]{1,0:T(8,128)(2,1)} async-done(((bf16[256,2048]{1,0:T(8,128)(2,1)}), bf16[256,512]{1,0:T(8,128)(2,1)}) %reduce-scatter.3.cloned.1.call-update) | async-done | bytes 262160 | tf_op jit(solution)/shard_map/reduce_scatter | solution.py:134
  (53 shorter events, 4.5 us)
Async XLA Ops:
  7.2 63.2 %copy-start = (bf16[256,2048]{1,0:T(8,128)(2,1)S(1)}, bf16[256,2048]{1,0:T(8,128)(2,1)}, u32[]{:S(2)}) copy-start(bf16[256,2048]{1,0:T(8,128)(2,1)} %param.6) | copy-start | bytes 3145732
  7.2 160.8 %reduce-scatter.5.cloned.1.call-start = ((), (), s32[]{:S(2)}) async-start(), calls=%async_computation.3 | async-start | bytes 7077888 | tf_op jit(solution)/shard_map/reduce_scatter | solution.py:138
  7.2 2.1 %collective-permute-start = (bf16[1,96,2048]{2,1,0:T(8,128)(2,1)}, bf16[1,96,2048]{2,1,0:T(8,128)(2,1)S(1)}, u32[]{:S(2)}, u32[]{:S(2)}) collective-permute-start(bf16[1,96,2048]{2,1,0:T(8,128)(2,1)} %param.7), channel_id=1, source_target_pairs={{0,4},{4,0},{8,12},{12,8},{16,20},{20,16},{24,28},{28,24},{1,5},{5... | collective-permute-start | bytes 1179656 | tf_op jit(solution)/shard_map/ppermute | solution.py:103
  7.8 28.2 %copy-start.3 = (bf16[256,512]{1,0:T(8,128)(2,1)S(1)}, bf16[256,512]{1,0:T(8,128)(2,1)}, u32[]{:S(2)}) copy-start(bf16[256,512]{1,0:T(8,128)(2,1)} %param.11) | copy-start | bytes 786436
  7.8 28.5 %copy-start.6 = (s32[256]{0:T(256)S(1)}, s32[256]{0:T(256)}, u32[]{:S(2)}) copy-start(s32[256]{0:T(256)} %param.10) | copy-start | bytes 3076
  11.6 20.9 %collective-permute-start.1 = (bf16[1,192,2048]{2,1,0:T(8,128)(2,1)}, bf16[1,192,2048]{2,1,0:T(8,128)(2,1)S(1)}, u32[]{:S(2)}, u32[]{:S(2)}) collective-permute-start(bf16[1,192,2048]{2,1,0:T(8,128)(2,1)} %maximum_select_fusion.4), channel_id=1, source_target_pairs={{0,8},{4,12},{8,0},{12,4},{16,24},{20,28},{24,16},{28,20},{1,9},{5... | collective-permute-start | bytes 2359304 | tf_op jit(solution)/shard_map/ppermute | solution.py:103
  34.2 36.2 %collective-permute-start.2 = (bf16[1,384,2048]{2,1,0:T(8,128)(2,1)}, bf16[1,384,2048]{2,1,0:T(8,128)(2,1)}, u32[]{:S(2)}, u32[]{:S(2)}) collective-permute-start(bf16[1,384,2048]{2,1,0:T(8,128)(2,1)} %maximum_select_fusion.2), channel_id=1, source_target_pairs={{0,16},{4,20},{8,24},{12,28},{16,0},{20,4},{24,8},{28,12},{1,17},{... | collective-permute-start | bytes 4718600 | tf_op jit(solution)/shard_map/ppermute | solution.py:103
  37.1 36.2 %copy-start.1 = (bf16[384,2048]{1,0:T(8,128)(2,1)}, bf16[384,2048]{1,0:T(8,128)(2,1)S(1)}, u32[]{:S(2)}) copy-start(bf16[384,2048]{1,0:T(8,128)(2,1)S(1)} %maximum_select_fusion.1) | copy-start | bytes 4718596
  70.4 3.1 %copy-start.5 = (f32[128]{0:T(128)S(1)}, f32[128]{0:T(128)}, u32[]{:S(2)}) copy-start(f32[128]{0:T(128)} %param.9) | copy-start | bytes 1540
  70.4 9.0 %copy-start.4 = (f32[128]{0:T(128)S(1)}, f32[128]{0:T(128)}, u32[]{:S(2)}) copy-start(f32[128]{0:T(128)} %param.8) | copy-start | bytes 1540
  74.1 5.7 %collective-permute-start.4 = (bf16[256,256]{0,1:T(8,128)(2,1)S(1)}, bf16[256,256]{0,1:T(8,128)(2,1)S(1)}, u32[]{:S(2)}, u32[]{:S(2)}) collective-permute-start(bf16[256,256]{0,1:T(8,128)(2,1)S(1)} %pad_maximum_fusion.2), channel_id=1, source_target_pairs={{0,4},{4,8},{8,12},{12,16},{16,20},{20,24},{24,28},{1,5},{5,9},{9,... | collective-permute-start | bytes 393224 | tf_op jit(solution)/shard_map/ppermute | solution.py:20
  75.4 7.2 %collective-permute-start.3 = (bf16[256,256]{0,1:T(8,128)(2,1)S(1)}, bf16[256,256]{0,1:T(8,128)(2,1)S(1)}, u32[]{:S(2)}, u32[]{:S(2)}) collective-permute-start(bf16[256,256]{0,1:T(8,128)(2,1)S(1)} %pad_maximum_fusion.2), channel_id=1, source_target_pairs={{0,8},{4,12},{8,16},{12,20},{16,24},{20,28},{1,9},{5,13},{9,17},{1... | collective-permute-start | bytes 393224 | tf_op jit(solution)/shard_map/ppermute | solution.py:20
  89.0 3.5 %collective-permute-start.5 = (bf16[256,256]{0,1:T(8,128)(2,1)S(1)}, bf16[256,256]{0,1:T(8,128)(2,1)S(1)}, u32[]{:S(2)}, u32[]{:S(2)}) collective-permute-start(bf16[256,256]{0,1:T(8,128)(2,1)S(1)} %get-tuple-element.10), channel_id=1, source_target_pairs={{4,0},{8,4},{12,8},{16,12},{20,16},{24,20},{28,24},{5,1},{9,5},{13... | collective-permute-start | bytes 393224 | tf_op jit(solution)/shard_map/ppermute | solution.py:20
  90.3 9.2 %collective-permute-start.6 = (bf16[256,256]{0,1:T(8,128)(2,1)S(1)}, bf16[256,256]{0,1:T(8,128)(2,1)S(1)}, u32[]{:S(2)}, u32[]{:S(2)}) collective-permute-start(bf16[256,256]{0,1:T(8,128)(2,1)S(1)} %get-tuple-element.11), channel_id=1, source_target_pairs={{8,0},{12,4},{16,8},{20,12},{24,16},{28,20},{9,1},{13,5},{17,9},{2... | collective-permute-start | bytes 393224 | tf_op jit(solution)/shard_map/ppermute | solution.py:20
  104.6 1.4 copy-start.2
  104.6 94.5 %reduce-scatter.3.cloned.1.call-start = ((), (), s32[]{:S(2)}) async-start(), calls=%async_computation.2 | async-start | bytes 1310720 | tf_op jit(solution)/shard_map/reduce_scatter | solution.py:134
  169.2 13.5 %collective-permute-start.7 = (bf16[96,2048]{1,0:T(8,128)(2,1)S(1)}, bf16[96,2048]{1,0:T(8,128)(2,1)S(1)}, u32[]{:S(2)}, u32[]{:S(2)}) collective-permute-start(bf16[96,2048]{1,0:T(8,128)(2,1)S(1)} %convert_element_type.61), channel_id=1, source_target_pairs={{0,1},{1,0},{2,3},{3,2},{4,5},{5,4},{6,7},{7,6},{8,9},{9,8},{10,11... | collective-permute-start | bytes 1179656 | tf_op jit(solution)/shard_map/ppermute | solution.py:24
Sparse Core Ops, SparseCore 0:
  104.8 63.2 reduce-scatter.4
  170.9 28.1 reduce-scatter.2
